TPU v7x, 512 devices: a whole 4x8x8 slice. The times are simulated.
512 devices in a mesh: dp: 32 (over z, x), seq: 16 (over y, core).
Axes of the slice: x: 4, y: 8, z: 8, core: 2. Of those that a mesh axis runs over, the one named last changes fastest.
Arguments:
- tokens: bfloat16 [32, 8192, 2048], P('dp', 'seq'), may hold values from -60 to 60
- in_gain: float32 [2048], replicated, may hold values from 0.1 to 1.9
- in_weight: bfloat16 [2048, 2304], P('dp'), may hold values from -0.125 to 0.125
- conv_weight: float32 [4, 2304], replicated, may hold values from -5 to 5
- conv_bias: float32 [2304], replicated, may hold values from -3 to 3
- log_decay: float32 [32, 32, 8192], P('dp', None, 'seq'), may hold values from -0.9 to 0
- skip: float32 [32], replicated, may hold values from 0.05 to 1
- out_gain: float32 [2048], replicated, may hold values from 0.1 to 1.9
- scan_order: int32 [512], replicated, may hold values from 0 to 511, each once
Outputs:
- regrouped: bfloat16 [32, 8192, 2048], P('dp', 'seq')
Inputs may be any that keep to these rules, and one draw needn't show every extreme that they name: Each of the 512 positions appears once; the q-th position of a frame in the next layer's scan is scan_order[q].
All inputs are finite; a program needn't handle non-finite values.
Results may differ from a plain program's by a relative error of at most 0.008.
Values may be sent and summed in bfloat16 or wider, within the bound.
No kernel may reach another device: no remote copies, remote signals or barrier semaphores. Data moves between devices by JAX's collectives and lax.ppermute only.
A program may use at most 128 MiB of HBM per device.

v0:
```python
import jax
import jax.numpy as jnp
from jax import lax
from jax.sharding import PartitionSpec as P

HALF_HEADS = 32
HEADDIM = 64
STATE = 128
GROUP = 128
POSITIONS = 512


def passed_along(block, axis, distance):
    devices = range(lax.axis_size(axis))
    route = [(i - distance, i) for i in devices if i - distance in devices]
    return lax.ppermute(block, axis, route)


def entering_2(part, axis, combine, identity):
    place = lax.axis_index(axis)
    gathered = jax.tree.map(lambda a: lax.all_gather(a, axis), part)
    state = jax.tree.map(lambda a, e: jnp.zeros_like(a) + jnp.asarray(e, a.dtype), part, identity)

    def one(step, state):
        return combine(
            state, jax.tree.map(lambda a: lax.dynamic_index_in_dim(a, step, 0, False), gathered)
        )

    return lax.fori_loop(0, place, one, state)


def project(operand, in_weight):
    whole_weight = lax.all_gather(in_weight, "dp", axis=0, tiled=True)
    return jnp.dot(operand, whole_weight, preferred_element_type=jnp.float32).astype(jnp.bfloat16)


def combine_states(earlier, later):
    return (earlier[0] * later[0], later[0][:, None, None] * earlier[1] + later[1])


def on_device(
    tokens, in_gain, in_weight, conv_weight, conv_bias, log_decay, skip, out_gain, scan_order
):
    own_tokens = tokens[0]
    token_count = own_tokens.shape[0]
    tap_count = conv_weight.shape[0]
    margin = tap_count - 1
    widened = own_tokens.astype(jnp.float32)
    inverse = lax.rsqrt(jnp.mean(widened * widened, axis=1, keepdims=True) + 1e-05)
    normed = (widened * inverse * in_gain[None, :]).astype(jnp.bfloat16)
    projected = project(normed, in_weight)
    earlier_rows = passed_along(projected[token_count - margin :], "seq", 1)
    extended = jnp.concatenate([earlier_rows, projected], axis=0)
    mixed_pre = conv_bias[None, :] + conv_weight[0][None, :] * extended[0:token_count].astype(
        jnp.float32
    )
    for offset in range(1, tap_count):
        mixed_pre = mixed_pre + conv_weight[offset][None, :] * extended[
            offset : offset + token_count
        ].astype(jnp.float32)
    mixed = jax.nn.silu(mixed_pre).astype(jnp.bfloat16)
    inner_width = HALF_HEADS * HEADDIM
    x_heads = mixed[:, :inner_width].reshape(token_count, HALF_HEADS, HEADDIM)
    b_vectors = mixed[:, inner_width : inner_width + STATE]
    c_vectors = mixed[:, inner_width + STATE :]
    own_decay = log_decay[0]
    block_count = token_count // GROUP
    places = jnp.arange(GROUP)
    causal = places[None, :] <= places[:, None]
    intra_parts = []
    block_states = []
    closings = []
    cumulatives = []
    device_state = jnp.zeros((HALF_HEADS, HEADDIM, STATE), jnp.float32)
    device_decay = jnp.ones((HALF_HEADS,), jnp.float32)
    for block_index in range(block_count):
        first_row = block_index * GROUP
        end_row = first_row + GROUP
        x_block = x_heads[first_row:end_row]
        b_block = b_vectors[first_row:end_row]
        c_block = c_vectors[first_row:end_row]
        decay_block = own_decay[:, first_row:end_row]
        cumulative = jnp.cumsum(decay_block, axis=1)
        step_size = -decay_block
        scores = lax.dot_general(
            c_block, b_block, (((1,), (1,)), ((), ())), preferred_element_type=jnp.float32
        )
        log_gap = cumulative[:, :, None] - cumulative[:, None, :]
        decay_mask = jnp.exp(jnp.where(causal[None], log_gap, -1e30))
        weights = (scores[None] * decay_mask * step_size[:, None, :]).astype(jnp.bfloat16)
        intra_parts.append(
            jnp.einsum("hts,shp->thp", weights, x_block, preferred_element_type=jnp.float32)
        )
        closing = cumulative[:, -1:]
        scaled = (
            (jnp.exp(closing - cumulative) * step_size).T[:, :, None] * x_block.astype(jnp.float32)
        ).astype(jnp.bfloat16)
        block_state = jnp.einsum("shp,sn->hpn", scaled, b_block, preferred_element_type=jnp.float32)
        fading = jnp.exp(closing[:, 0])
        device_state = fading[:, None, None] * device_state + block_state
        device_decay = device_decay * fading
        block_states.append(block_state)
        closings.append(fading)
        cumulatives.append(cumulative)
    carried = entering_2(
        (device_decay, device_state),
        "seq",
        combine_states,
        (jnp.ones_like(device_decay), jnp.zeros_like(device_state)),
    )
    entering = carried[1]
    outputs = []
    for block_index in range(block_count):
        first_row = block_index * GROUP
        c_block = c_vectors[first_row : first_row + GROUP]
        inter = jnp.einsum(
            "tn,hpn->thp",
            c_block,
            entering.astype(jnp.bfloat16),
            preferred_element_type=jnp.float32,
        )
        inter = inter * jnp.exp(cumulatives[block_index]).T[:, :, None]
        outputs.append(intra_parts[block_index] + inter)
        entering = closings[block_index][:, None, None] * entering + block_states[block_index]
    ssm_out = jnp.concatenate(outputs, axis=0) + skip[None, :, None] * x_heads.astype(jnp.float32)
    head_scale = lax.rsqrt(jnp.mean(ssm_out * ssm_out, axis=2, keepdims=True) + 1e-05)
    normalized = (ssm_out * head_scale * out_gain.reshape(HALF_HEADS, HEADDIM)[None]).astype(
        jnp.bfloat16
    )
    frames_here = token_count // POSITIONS
    framed = normalized.reshape(frames_here, POSITIONS, inner_width)
    picked = jnp.take(framed, scan_order, axis=1).transpose(1, 0, 2)
    seq_count = lax.axis_size("seq")
    outgoing = picked.reshape(seq_count, POSITIONS // seq_count, frames_here, inner_width)
    arrived = lax.all_to_all(outgoing, "seq", split_axis=0, concat_axis=2, tiled=True)
    return arrived.reshape(1, token_count, inner_width)


def solution(mesh):
    in_specs = (
        P("dp", "seq", None),
        P(),
        P("dp", None),
        P(),
        P(),
        P("dp", None, "seq"),
        P(),
        P(),
        P(),
    )
    out_specs = P("dp", "seq", None)
    return jax.shard_map(
        on_device, mesh=mesh, in_specs=in_specs, out_specs=out_specs, check_vma=False
    )
```

profile of v0, /device:TPU:1, one launch (start us, length us, event | category | flops | bytes accessed | tf_op | source)
XLA Modules:
  0.0 378.1 jit_solution(2298110102641624891)
XLA Ops:
  10.5 2.1 fusion
  13.3 111.3 %all-gather.5.cloned.1.call-done = bf16[2048,2304]{1,0:T(8,128)(2,1)} async-done(((bf16[64,2304]{1,0:T(8,128)(2,1)}), bf16[2048,2304]{1,0:T(8,128)(2,1)}) %all-gather.5.cloned.1.call-update) | async-done | bytes 9437200 | tf_op jit(solution)/shard_map/all_gather | solution.py:33
  124.6 9.1 %convolution_convert_fusion = bf16[512,2304]{1,0:T(8,128)(2,1)S(1)} fusion(bf16[2048,2304]{1,0:T(8,128)(2,1)} %all-gather.5.cloned.1.call-done, bf16[1,512,2048]{2,1,0:T(8,128)(2,1)S(1)} %copy-done.15, f32[2048]{0:T(1024)S(1)} %copy-done.41, f32[512]{0:T(512)S(1)} %add_rsqrt_fusion.1), kind=kOutput, calls=%fused_computation.6 | convolution fusion | flops 4837212160 | bytes 13903872 | tf_op jit(solution)/shard_map/dot_general | solution.py:34
  133.8 4.4 %collective-permute-start = (bf16[3,2304]{1,0:T(4,128)(2,1)S(1)}, bf16[3,2304]{1,0:T(4,128)(2,1)S(1)}, u32[]{:S(2)}, u32[]{:S(2)}) collective-permute-start(bf16[3,2304]{1,0:T(4,128)(2,1)S(1)} %slice.152), channel_id=1, source_target_pairs={{0,1},{1,2},{2,3},{3,4},{4,5},{5,6},{6,7},{7,8},{8,9},{9,10},{10,1... | collective-permute-start | bytes 41480 | tf_op jit(solution)/shard_map/ppermute | solution.py:16
  140.0 3.4 multiply_convert_fusion
  143.4 1.5 fusion.85
  144.9 2.0 copy.46
  148.2 1.3 copy.49
  149.6 1.3 fusion.42
  150.9 1.7 fusion.43
  154.1 1.4 convolution_add_fusion
  158.2 24.8 %all-reduce = f32[512]{0:T(512)S(1)} all-reduce(f32[512]{0:T(512)S(1)} %dynamic-update-slice), channel_id=2, replica_groups=mesh['dp'=32,'seq'=16] {'seq'}, use_global_device_ids=true, to_apply=%add | all-reduce | flops 512 | bytes 4096
  188.3 2.5 slice_convert_fusion
  190.8 5.4 %copy.54 = f32[512,2048]{0,1:T(8,128)} copy(f32[512,2048]{1,0:T(8,128)} %slice_convert_fusion) | data formatting | bytes 8388608 | tf_op jit(solution)/shard_map/convert_element_type | solution.py:125
  196.8 3.0 convolution_bitcast_fusion.3
  199.8 1.9 convolution_bitcast_fusion.2
  201.7 1.9 convolution_bitcast_fusion.1
  203.6 1.9 convolution_bitcast_fusion
  205.5 45.8 %all-gather.7.cloned.1.call-done = f32[512,64,128]{2,1,0:T(8,128)} async-done(((f32[32,64,128]{2,1,0:T(8,128)}), f32[512,64,128]{2,1,0:T(8,128)}) %all-gather.7.cloned.1.call-update) | async-done | bytes 16777232 | tf_op jit(solution)/shard_map/all_gather | solution.py:21
  251.4 2.3 while.12
  252.1 1.4 bitcast_add_fusion.2
  253.8 1.9 multiply_add_fusion
  262.2 2.5 mul.426
  264.7 5.5 %copy.55 = f32[512,2048]{1,0:T(8,128)} copy(f32[512,2048]{0,1:T(8,128)} %bitcast.90) | data formatting | bytes 8388608 | tf_op jit(solution)/shard_map/mul | solution.py:127
  270.2 1.3 copy.50
  271.6 1.3 copy.51
  274.2 1.3 copy.53
  275.6 4.3 %fusion.5 = bf16[512,2048]{1,0:T(8,128)(2,1)S(1)} fusion(f32[512,2048]{1,0:T(8,128)} %copy.55, f32[128,2048]{1,0:T(8,128)} %copy.53, f32[128,2048]{1,0:T(8,128)} %copy.52, f32[128,2048]{1,0:T(8,128)} %copy.51, f32[128,2048]{1,0:T(8,128)S(1)} %copy-done.13, f32[2048]{0:T(1024)S(1)} %copy-done.31, f32[2048]{0:T(1024)S(1)} %copy-done.23, ...), kind=kLoop, calls=%fused_computation.13 | loop fusion | flops 9437184 | bytes 12599296 | tf_op jit(solution)/shard_map/convert_element_type | solution.py:127
  279.9 3.3 gather_fusion
  283.2 1.8 broadcast_select_fusion
  285.1 83.7 %all_to_all.15 = bf16[16,32,1,2048]{3,1,2,0:T(8,128)(2,1)S(1)} all-to-all(bf16[16,32,1,2048]{3,1,2,0:T(8,128)(2,1)S(1)} %broadcast_select_fusion), channel_id=1, replica_groups=mesh['dp'=32,'seq'=16] {'seq'}, dimensions={0} | all-to-all | bytes 4194304 | tf_op jit(solution)/shard_map/all_to_all | solution.py:135
  368.8 2.5 copy.57
  (130 shorter events, 25.6 us)
Async XLA Ops:
  6.5 6.1 %copy-start.20 = (f32[1,32,512]{2,1,0:T(8,128)S(1)}, f32[1,32,512]{2,1,0:T(8,128)}, u32[]{:S(2)}) copy-start(f32[1,32,512]{2,1,0:T(8,128)} %param.16) | copy-start | bytes 196612
  6.5 118.1 %copy-start.15 = (bf16[1,512,2048]{2,1,0:T(8,128)(2,1)S(1)}, bf16[1,512,2048]{2,1,0:T(8,128)(2,1)}, u32[]{:S(2)}) copy-start(bf16[1,512,2048]{2,1,0:T(8,128)(2,1)} %param.11) | copy-start | bytes 6291460
  6.5 118.1 %copy-start.41 = (f32[2048]{0:T(1024)S(1)}, f32[2048]{0:T(1024)}, u32[]{:S(2)}) copy-start(f32[2048]{0:T(1024)} %param.12) | copy-start | bytes 24580
  6.5 118.1 %all-gather.5.cloned.1.call-start = ((), (), s32[]{:S(2)}) async-start(), calls=%async_computation.1 | async-start | bytes 9732096 | tf_op jit(solution)/shard_map/all_gather | solution.py:33
  7.3 244.0 %all-gather.7.cloned.1.call-start = ((), (), s32[]{:S(2)}) async-start(), calls=%async_computation.2 | async-start | bytes 17825792 | tf_op jit(solution)/shard_map/all_gather | solution.py:21
  13.3 124.8 %copy-start.22 = (f32[4,2304]{1,0:T(4,128)S(1)}, f32[4,2304]{1,0:T(4,128)}, u32[]{:S(2)}) copy-start(f32[4,2304]{1,0:T(4,128)} %param.14) | copy-start | bytes 110596
  13.3 126.7 %copy-start.29 = (f32[2304]{0:T(1024)S(1)}, f32[2304]{0:T(1024)}, u32[]{:S(2)}) copy-start(f32[2304]{0:T(1024)} %param.15) | copy-start | bytes 27652
  133.8 6.2 %collective-permute-start = (bf16[3,2304]{1,0:T(4,128)(2,1)S(1)}, bf16[3,2304]{1,0:T(4,128)(2,1)S(1)}, u32[]{:S(2)}, u32[]{:S(2)}) collective-permute-start(bf16[3,2304]{1,0:T(4,128)(2,1)S(1)} %slice.152), channel_id=1, source_target_pairs={{0,1},{1,2},{2,3},{3,4},{4,5},{5,6},{6,7},{7,8},{8,9},{9,10},{10,1... | collective-permute-start | bytes 41480 | tf_op jit(solution)/shard_map/ppermute | solution.py:16
  143.3 115.0 %copy-start = (bf16[512,2304]{1,0:T(8,128)(2,1)}, bf16[512,2304]{1,0:T(8,128)(2,1)S(1)}, u32[]{:S(2)}) copy-start(bf16[512,2304]{1,0:T(8,128)(2,1)S(1)} %multiply_convert_fusion) | copy-start | bytes 7077892
  149.5 3.1 copy-start.21
  149.5 4.5 %copy-start.34 = (f32[32]{0:T(128)S(1)}, f32[32]{0:T(128)}, u32[]{:S(2)}) copy-start(f32[32]{0:T(128)} %exp.131) | copy-start | bytes 388
  149.5 4.5 %copy-start.36 = (f32[32]{0:T(128)S(1)}, f32[32]{0:T(128)}, u32[]{:S(2)}) copy-start(f32[32]{0:T(128)} %exp.132) | copy-start | bytes 388
  149.6 4.5 %copy-start.39 = (f32[32]{0:T(128)S(1)}, f32[32]{0:T(128)}, u32[]{:S(2)}) copy-start(f32[32]{0:T(128)} %get-tuple-element.90) | copy-start | bytes 388
  149.6 4.5 %copy-start.40 = (f32[32]{0:T(128)S(1)}, f32[32]{0:T(128)}, u32[]{:S(2)}) copy-start(f32[32]{0:T(128)} %exp.130) | copy-start | bytes 388
  150.9 2.1 copy-start.1
  190.8 6.0 %copy-start.27 = (f32[32,128]{1,0:T(8,128)S(1)}, f32[32,128]{1,0:T(8,128)}, u32[]{:S(2)}) copy-start(f32[32,128]{1,0:T(8,128)} %get-tuple-element.73) | copy-start | bytes 49156
  196.2 3.6 copy-start.14
  196.2 3.6 copy-start.26
  196.2 3.6 copy-start.28
  251.4 2.4 copy-start.33
  251.4 2.4 copy-start.37
  256.0 4.3 %copy-start.4 = (f32[128,32,64]{0,2,1:T(8,128)}, f32[128,32,64]{0,2,1:T(8,128)S(1)}, u32[]{:S(2)}) copy-start(f32[128,32,64]{0,2,1:T(8,128)S(1)} %fusion.17) | copy-start | bytes 3145732
  256.0 2.0 copy-start.19
  258.0 2.3 copy-start.6
  258.3 2.9 copy-start.3
  258.3 2.8 copy-start.38
  264.7 5.5 %copy-start.5 = (f32[128,32,64]{0,2,1:T(8,128)S(1)}, f32[128,32,64]{0,2,1:T(8,128)}, u32[]{:S(2)}) copy-start(f32[128,32,64]{0,2,1:T(8,128)} %copy-done.4) | copy-start | bytes 3145732
  271.6 2.7 copy-start.9
  272.9 2.6 copy-start.23
  272.9 2.6 copy-start.31
  275.6 4.3 %copy-start.30 = (s32[1024]{0:T(1024)S(1)}, s32[1024]{0:T(1024)}, u32[]{:S(2)}) copy-start(s32[1024]{0:T(1024)} %pad_clamp_fusion) | copy-start | bytes 12292
  279.9 3.3 copy-start.32
  (13 other events, 20.1 us)
Sparse Core Ops, SparseCore 0:
  10.5 114.0 all-gather.4
  155.6 95.6 all-gather.6
where the time goes:
time: 380 us; the launch traced here: 378 us
  waiting for transfers between devices  158 us (42%)
  blocking collectives  108 us (28%)
  local copies, waits for them, and re-layouts  44 us (12%)
  matrix products  24.4 us (6%)
  other arithmetic  24.2 us (6%)
  between operations  14.5 us (4%)
  starting transfers between devices  4.43 us (1%)
    all_gather x1, waiting for transfers between devices, project(): whole_weight = lax.all_gather(in_weight, 'dp', axis=0, tiled=True)  111 us
    all_to_all x1, blocking collectives, on_device(): lax.all_to_all(outgoing, 'seq', split_axis=0, concat_axis=2, tiled=True)  83.7 us
    all_gather x1, waiting for transfers between devices, entering_2(): gathered = jax.tree.map(lambda a: lax.all_gather(a, axis), part)  45.8 us
    unnamed x1, blocking collectives  24.8 us
    dot_general x1, matrix products, project(): jnp.dot(operand, whole_weight, preferred_element_type=jnp.float32)  9.08 us
    dot_general x4, matrix products, on_device(): jnp.einsum('hts,shp->thp', weights, x_block, preferred_element_type=jnp.f...  8.69 us
    mul x2, local copies, waits for them, and re-layouts, on_device(): ssm_out * head_scale * out_gain.reshape(HALF_HEADS, HEADDIM)[None]  8.02 us
  transfers between devices with their start and end apart: 3, of which 2 were waited for; matrix products, arithmetic and copies ran while one was open for 9% of the time, Pallas kernels for 0%

commit v1 on v0

--- a/solution.py
+++ b/solution.py
@@ -30,7 +30,10 @@
 
 
 def project(operand, in_weight):
-    whole_weight = lax.all_gather(in_weight, "dp", axis=0, tiled=True)
+    devices_2 = lax.axis_size("dp")
+    blocks = jnp.stack([in_weight for _ in range(devices_2)])
+    blocks = lax.all_to_all(blocks, "dp", split_axis=0, concat_axis=0)
+    whole_weight = jnp.concatenate(blocks, axis=0)
     return jnp.dot(operand, whole_weight, preferred_element_type=jnp.float32).astype(jnp.bfloat16)
 
 

time: 380 us -> 506 us (1.33)
  waiting for transfers between devices: 158 us -> 268 us
  starting transfers between devices: 4.43 us -> 18.8 us
    all_to_all x0 -> x1, waiting for transfers between devices: none -> 207 us  [project(): blocks = lax.all_to_all(blocks, 'dp', split_axis=0, concat_axis=0)]
    all_gather x1 -> x0, waiting for transfers between devices: 111 us -> none  [project(): whole_weight = lax.all_gather(in_weight, 'dp', axis=0, tiled=True)]
    all_gather x1, waiting for transfers between devices: 45.8 us -> 60.5 us  [entering_2(): gathered = jax.tree.map(lambda a: lax.all_gather(a, axis), part)]
    all_to_all x0 -> x1, starting transfers between devices: none -> 13.9 us  [project(): blocks = lax.all_to_all(blocks, 'dp', split_axis=0, concat_axis=0)]
    another operation x1 -> x2, local copies, waits for them, and re-layouts: 0.11 us -> 5.78 us  [the longest x1 5.68 us: project(): blocks = jnp.stack([in_weight for _ in range(devices_2)])]
  transfers between devices with their start and end apart: 3 -> 3, of which waited for: 2 -> 2; matrix products, arithmetic and copies ran while one was open for 9% -> 6% of each run, Pallas kernels for 0% -> 0%
where the time goes in v1:
time: 506 us; the launch traced here: 505 us
  waiting for transfers between devices  268 us (53%)
  blocking collectives  108 us (21%)
  local copies, waits for them, and re-layouts  48.9 us (10%)
  matrix products  24.4 us (5%)
  other arithmetic  22.6 us (4%)
  starting transfers between devices  18.8 us (4%)
  between operations  14.5 us (3%)
    all_to_all x1, waiting for transfers between devices, project(): blocks = lax.all_to_all(blocks, 'dp', split_axis=0, concat_axis=0)  207 us
    all_to_all x1, blocking collectives, on_device(): lax.all_to_all(outgoing, 'seq', split_axis=0, concat_axis=2, tiled=True)  83.9 us
    all_gather x1, waiting for transfers between devices, entering_2(): gathered = jax.tree.map(lambda a: lax.all_gather(a, axis), part)  60.5 us
    unnamed x1, blocking collectives  23.8 us
    all_to_all x1, starting transfers between devices, project(): blocks = lax.all_to_all(blocks, 'dp', split_axis=0, concat_axis=0)  13.9 us
  transfers between devices with their start and end apart: 3, of which 2 were waited for; matrix products, arithmetic and copies ran while one was open for 6% of the time, Pallas kernels for 0%

profile of v1, /device:TPU:1, one launch (start us, length us, event | category | flops | bytes accessed | tf_op | source)
XLA Modules:
  0.0 504.6 jit_solution(2698913618406828252)
XLA Ops:
  6.5 5.7 %stack.2 = bf16[32,64,2304]{2,1,0:T(8,128)(2,1)} broadcast(bf16[64,2304]{1,0:T(8,128)(2,1)} %param.13), dimensions={1,2} | broadcast | bytes 9732096 | tf_op jit(solution)/shard_map/stack | solution.py:34
  12.2 13.9 %all-to-all-start = ((bf16[32,64,2304]{2,1,0:T(8,128)(2,1)}), bf16[32,64,2304]{2,1,0:T(8,128)(2,1)}, u32[]{:S(2)}, u32[]{:S(2)}) async-start(bf16[32,64,2304]{2,1,0:T(8,128)(2,1)} %stack.2), calls=%async_computation | async-start | bytes 18874368 | tf_op jit(solution)/shard_map/all_to_all | solution.py:35
  29.9 207.0 %all-to-all-done = bf16[32,64,2304]{2,1,0:T(8,128)(2,1)} async-done(((bf16[32,64,2304]{2,1,0:T(8,128)(2,1)}), bf16[32,64,2304]{2,1,0:T(8,128)(2,1)}, u32[]{:S(2)}, u32[]{:S(2)}) %all-to-all-start) | async-done | bytes 9437216 | tf_op jit(solution)/shard_map/all_to_all | solution.py:35
  236.9 9.1 %convolution_convert_fusion = bf16[512,2304]{1,0:T(8,128)(2,1)S(1)} fusion(bf16[2048,2304]{1,0:T(8,128)(2,1)} %bitcast.3, bf16[1,512,2048]{2,1,0:T(8,128)(2,1)S(1)} %copy-done.15, f32[2048]{0:T(1024)S(1)} %copy-done.41, f32[512]{0:T(512)S(1)} %add_rsqrt_fusion.1), kind=kOutput, calls=%fused_computation.6 | convolution fusion | flops 4837212160 | bytes 13903872 | tf_op jit(solution)/shard_map/dot_general | solution.py:37
  246.1 4.8 collective-permute-start
  252.6 3.4 multiply_convert_fusion
  255.9 1.5 fusion.85
  257.5 2.0 copy.46
  260.8 1.3 copy.49
  262.2 1.3 fusion.42
  263.5 1.7 fusion.43
  266.6 1.4 convolution_add_fusion
  270.7 23.8 %all-reduce = f32[512]{0:T(512)S(1)} all-reduce(f32[512]{0:T(512)S(1)} %dynamic-update-slice), channel_id=2, replica_groups=mesh['dp'=32,'seq'=16] {'seq'}, use_global_device_ids=true, to_apply=%add | all-reduce | flops 512 | bytes 4096
  299.8 2.5 slice_convert_fusion
  302.4 5.5 %copy.54 = f32[512,2048]{0,1:T(8,128)} copy(f32[512,2048]{1,0:T(8,128)} %slice_convert_fusion) | data formatting | bytes 8388608 | tf_op jit(solution)/shard_map/convert_element_type | solution.py:128
  308.4 3.0 convolution_bitcast_fusion.3
  311.4 1.9 convolution_bitcast_fusion.2
  313.4 1.9 convolution_bitcast_fusion.1
  315.3 1.9 convolution_bitcast_fusion
  317.2 60.5 %all-gather.4.cloned.1.call-done = f32[512,64,128]{2,1,0:T(8,128)} async-done(((f32[32,64,128]{2,1,0:T(8,128)}), f32[512,64,128]{2,1,0:T(8,128)}) %all-gather.4.cloned.1.call-update) | async-done | bytes 16777232 | tf_op jit(solution)/shard_map/all_gather | solution.py:21
  377.8 2.4 while.12
  378.6 1.4 bitcast_add_fusion.2
  380.2 1.9 multiply_add_fusion
  388.6 2.5 mul.429
  391.2 5.5 %copy.55 = f32[512,2048]{1,0:T(8,128)} copy(f32[512,2048]{0,1:T(8,128)} %bitcast.87) | data formatting | bytes 8388608 | tf_op jit(solution)/shard_map/mul | solution.py:130
  396.6 1.3 copy.50
  398.0 1.3 copy.51
  401.9 4.3 fusion.5
  406.3 3.3 gather_fusion
  409.6 1.8 broadcast_select_fusion
  411.4 83.9 %all_to_all.20 = bf16[16,32,1,2048]{3,1,2,0:T(8,128)(2,1)S(1)} all-to-all(bf16[16,32,1,2048]{3,1,2,0:T(8,128)(2,1)S(1)} %broadcast_select_fusion), channel_id=1, replica_groups=mesh['dp'=32,'seq'=16] {'seq'}, dimensions={0} | all-to-all | bytes 4194304 | tf_op jit(solution)/shard_map/all_to_all | solution.py:138
  495.3 2.5 copy.57
  (130 shorter events, 25.8 us)
Async XLA Ops:
  12.2 14.0 %copy-start.20 = (f32[1,32,512]{2,1,0:T(8,128)S(1)}, f32[1,32,512]{2,1,0:T(8,128)}, u32[]{:S(2)}) copy-start(f32[1,32,512]{2,1,0:T(8,128)} %param.16) | copy-start | bytes 196612
  12.2 16.5 %copy-start.15 = (bf16[1,512,2048]{2,1,0:T(8,128)(2,1)S(1)}, bf16[1,512,2048]{2,1,0:T(8,128)(2,1)}, u32[]{:S(2)}) copy-start(bf16[1,512,2048]{2,1,0:T(8,128)(2,1)} %param.11) | copy-start | bytes 6291460
  12.2 224.7 %all-to-all-start = ((bf16[32,64,2304]{2,1,0:T(8,128)(2,1)}), bf16[32,64,2304]{2,1,0:T(8,128)(2,1)}, u32[]{:S(2)}, u32[]{:S(2)}) async-start(bf16[32,64,2304]{2,1,0:T(8,128)(2,1)} %stack.2), calls=%async_computation | async-start | bytes 18874368 | tf_op jit(solution)/shard_map/all_to_all | solution.py:35
  26.2 210.7 %copy-start.41 = (f32[2048]{0:T(1024)S(1)}, f32[2048]{0:T(1024)}, u32[]{:S(2)}) copy-start(f32[2048]{0:T(1024)} %param.12) | copy-start | bytes 24580
  26.2 351.5 %all-gather.4.cloned.1.call-start = ((), (), s32[]{:S(2)}) async-start(), calls=%async_computation.2 | async-start | bytes 17825792 | tf_op jit(solution)/shard_map/all_gather | solution.py:21
  236.9 14.0 %copy-start.22 = (f32[4,2304]{1,0:T(4,128)S(1)}, f32[4,2304]{1,0:T(4,128)}, u32[]{:S(2)}) copy-start(f32[4,2304]{1,0:T(4,128)} %param.14) | copy-start | bytes 110596
  236.9 15.6 %copy-start.29 = (f32[2304]{0:T(1024)S(1)}, f32[2304]{0:T(1024)}, u32[]{:S(2)}) copy-start(f32[2304]{0:T(1024)} %param.15) | copy-start | bytes 27652
  246.1 6.5 %collective-permute-start = (bf16[3,2304]{1,0:T(4,128)(2,1)S(1)}, bf16[3,2304]{1,0:T(4,128)(2,1)S(1)}, u32[]{:S(2)}, u32[]{:S(2)}) collective-permute-start(bf16[3,2304]{1,0:T(4,128)(2,1)S(1)} %slice.152), channel_id=1, source_target_pairs={{0,1},{1,2},{2,3},{3,4},{4,5},{5,6},{6,7},{7,8},{8,9},{9,10},{10,1... | collective-permute-start | bytes 41480 | tf_op jit(solution)/shard_map/ppermute | solution.py:16
  255.9 128.8 %copy-start = (bf16[512,2304]{1,0:T(8,128)(2,1)}, bf16[512,2304]{1,0:T(8,128)(2,1)S(1)}, u32[]{:S(2)}) copy-start(bf16[512,2304]{1,0:T(8,128)(2,1)S(1)} %multiply_convert_fusion) | copy-start | bytes 7077892
  262.1 3.1 copy-start.21
  262.1 4.5 copy-start.34
  262.1 4.5 copy-start.36
  262.1 4.5 copy-start.39
  262.2 4.5 copy-start.40
  263.5 2.1 copy-start.1
  302.4 6.1 %copy-start.27 = (f32[32,128]{1,0:T(8,128)S(1)}, f32[32,128]{1,0:T(8,128)}, u32[]{:S(2)}) copy-start(f32[32,128]{1,0:T(8,128)} %get-tuple-element.73) | copy-start | bytes 49156
  307.8 3.6 copy-start.14
  307.8 3.6 copy-start.26
  307.8 3.6 copy-start.28
  377.8 2.4 copy-start.33
  377.8 2.4 copy-start.37
  382.4 4.3 copy-start.4
  382.4 2.0 copy-start.19
  384.4 2.3 copy-start.6
  384.7 2.9 copy-start.3
  384.7 2.9 copy-start.38
  391.1 5.5 %copy-start.5 = (f32[128,32,64]{0,2,1:T(8,128)S(1)}, f32[128,32,64]{0,2,1:T(8,128)}, u32[]{:S(2)}) copy-start(f32[128,32,64]{0,2,1:T(8,128)} %copy-done.4) | copy-start | bytes 3145732
  398.0 2.7 copy-start.9
  399.3 2.6 copy-start.23
  399.3 2.6 copy-start.31
  401.9 4.4 copy-start.30
  406.3 3.3 copy-start.32
  (13 other events, 20.1 us)
Sparse Core Ops, SparseCore 0:
  268.1 109.5 all-gather.3
